TPU v7x, 32 devices: a whole 2x2x4 slice. The times are simulated.
32 devices in a mesh: cfg: 2 (over y), space: 16 (over z, x, core).
Axes of the slice: x: 2, y: 2, z: 4, core: 2. Of those that a mesh axis runs over, the one named last changes fastest.
Arguments:
- vectors: bfloat16 [2, 3, 128, 16384], P(None, None, None, ('cfg', 'space')), parts along dimension 3, may hold values from -12 to 12
- links: bfloat16 [3, 2, 3, 3, 16384], P(None, None, None, None, ('cfg', 'space')), parts along dimension 4, may hold values from -2.5 to 2.5
- momenta: int32 [8, 3], replicated, may hold values from -2 to 2, as said below
- displacements: int32 [8], replicated, may hold values from 0 to 2
- perambulators: bfloat16 [4, 2, 128, 32768], P(None, None, None, ('cfg', 'space')), parts along dimension 3, may hold values from -0.059814453 to 0.059814453
Outputs:
- smeared: bfloat16 [2, 3, 128, 16384], P(None, None, None, ('cfg', 'space')), parts along dimension 3
- correlator: float32 [4, 8, 256], P(None, None, ('cfg', 'space')), parts along dimension 2
There are 2 independent parts, one for each index of `cfg`. A program takes and returns all parts, laid end to end along the dimension named above; an argument that names none is the same for every part. Nothing has to cross between parts.
Inputs may be any that keep to these rules, and one draw needn't show every extreme that they name: `momenta`: the first component of every momentum is nonzero.
All inputs are finite; a program needn't handle non-finite values.
Results may differ from a plain program's by a relative error of at most 0.0091.
Values may be sent and summed in bfloat16 or wider, within the bound.
No kernel may reach another device: no remote copies, remote signals or barrier semaphores. Data moves between devices by JAX's collectives and lax.ppermute only.
A program may use at most 128 MiB of HBM per device.

v0:
```python
import math

import jax
import jax.numpy as jnp
from jax import lax
from jax.sharding import PartitionSpec as P

TG = 8
LX = 16
LY = 16
HOPS = 4


KAPPA = 0.1


def passed_along(shard, axis, by):
    peers = lax.axis_size(axis)
    return lax.ppermute(shard, axis, [(i, (i + by) % peers) for i in range(peers)])


def partner_2(shard, axis, apart):
    return lax.ppermute(shard, axis, [(i, i ^ 1 << apart) for i in range(lax.axis_size(axis))])


def link_apply(link_re, link_im, vec_re, vec_im, adjoint):
    outs_re = []
    outs_im = []
    for colour_out in range(3):
        total_re = None
        total_im = None
        for colour_in in range(3):
            if adjoint:
                mat_re = link_re[colour_in, colour_out]
                mat_im = -link_im[colour_in, colour_out]
            else:
                mat_re = link_re[colour_out, colour_in]
                mat_im = link_im[colour_out, colour_in]
            term_re = mat_re[None] * vec_re[colour_in] - mat_im[None] * vec_im[colour_in]
            term_im = mat_re[None] * vec_im[colour_in] + mat_im[None] * vec_re[colour_in]
            if total_re is None:
                total_re, total_im = (term_re, term_im)
            else:
                total_re = total_re + term_re
                total_im = total_im + term_im
        outs_re.append(total_re)
        outs_im.append(total_im)
    return (jnp.stack(outs_re), jnp.stack(outs_im))


def phase_angle(momentum, coord_x, coord_y, coord_z, extent_z):
    frac = (momentum[0] * coord_x % LX).astype(jnp.float32) / LX
    frac = frac + (momentum[1] * coord_y % LY).astype(jnp.float32) / LY
    frac = frac + (momentum[2] * coord_z % extent_z).astype(jnp.float32) / extent_z
    return 2.0 * math.pi * frac


def beside(field, axis_code, offset):
    last = field.ndim - 1
    if axis_code == 1:
        return jnp.roll(field, -offset * LX, last)
    column = lax.broadcasted_iota(jnp.int32, (field.shape[-1],), 0) % LX
    if offset > 0:
        return jnp.where(column == LX - 1, jnp.roll(field, LX - 1, last), jnp.roll(field, -1, last))
    return jnp.where(column == 0, jnp.roll(field, 1 - LX, last), jnp.roll(field, 1, last))


def smear_block(v_ext, links_here, z_below):
    centre = v_ext[:, :, :, 1:-1]
    total_re = (1.0 - 6.0 * KAPPA) * centre[0]
    total_im = (1.0 - 6.0 * KAPPA) * centre[1]
    for axis_code in range(2):
        link = links_here[axis_code]
        ahead_re, ahead_im = link_apply(
            link[0],
            link[1],
            beside(centre[0], axis_code, 1),
            beside(centre[1], axis_code, 1),
            False,
        )
        behind = beside(link, axis_code, -1)
        back_re, back_im = link_apply(
            behind[0],
            behind[1],
            beside(centre[0], axis_code, -1),
            beside(centre[1], axis_code, -1),
            True,
        )
        total_re = total_re + KAPPA * (ahead_re + back_re)
        total_im = total_im + KAPPA * (ahead_im + back_im)
    link = links_here[2]
    ahead_re, ahead_im = link_apply(link[0], link[1], v_ext[0, :, :, 2:], v_ext[1, :, :, 2:], False)
    behind = jnp.concatenate([z_below, link[:, :, :, :-1]], axis=3)
    back_re, back_im = link_apply(
        behind[0], behind[1], v_ext[0, :, :, :-2], v_ext[1, :, :, :-2], True
    )
    total_re = total_re + KAPPA * (ahead_re + back_re)
    total_im = total_im + KAPPA * (ahead_im + back_im)
    return jnp.stack([total_re, total_im])


def from_below(payload):
    return passed_along(payload, "space", TG)


def from_above(payload):
    return passed_along(payload, "space", -TG)


def partner(values, bit_place):
    return partner_2(values, "space", bit_place)


def body(vectors, links, momenta, displacements, perambulators):
    vector_count = vectors.shape[2]
    plane = LX * LY
    depth = vectors.shape[3] // plane
    blocks = lax.axis_size("space") // TG
    block = lax.axis_index("space") // TG
    field = vectors.reshape(2, 3, vector_count, depth, plane)
    lattice = links.reshape(3, 2, 3, 3, depth, plane)
    wide_links = lattice.astype(jnp.float32)
    rows_vec = 6 * vector_count
    current = field
    for sweep in range(2):
        lower = from_below(
            jnp.concatenate(
                [
                    current[:, :, :, -1:].reshape(-1, plane),
                    lattice[2, :, :, :, -1:].reshape(-1, plane),
                ],
                axis=0,
            )
        )
        upper = from_above(current[:, :, :, :1].reshape(-1, plane))
        v_ext = jnp.concatenate(
            [
                lower[:rows_vec].reshape(2, 3, vector_count, 1, plane),
                current,
                upper.reshape(2, 3, vector_count, 1, plane),
            ],
            axis=3,
        ).astype(jnp.float32)
        z_below = lower[rows_vec:].reshape(2, 3, 3, 1, plane).astype(jnp.float32)
        current = smear_block(v_ext, wide_links, z_below).astype(jnp.bfloat16)
    smeared = current
    upper = from_above(smeared[:, :, :, :1].reshape(-1, plane)).reshape(
        2, 3, vector_count, 1, plane
    )
    wide = smeared.astype(jnp.float32)
    raised = jnp.concatenate([smeared, upper], axis=3)[:, :, :, 1:].astype(jnp.float32)
    moved = []
    for axis_code in range(3):
        link = wide_links[axis_code]
        if axis_code < 2:
            ahead_re = beside(wide[0], axis_code, 1)
            ahead_im = beside(wide[1], axis_code, 1)
        else:
            ahead_re = raised[0]
            ahead_im = raised[1]
        moved_re, moved_im = link_apply(link[0], link[1], ahead_re, ahead_im, False)
        moved.append(jnp.stack([moved_re, moved_im]).astype(jnp.bfloat16))
    displaced = jnp.stack(moved)
    position = lax.broadcasted_iota(jnp.int32, (depth, plane), 1)
    coord_x = position % LX
    coord_y = position // LX
    coord_z = lax.broadcasted_iota(jnp.int32, (depth, plane), 0) + block * depth
    extent_z = depth * blocks
    scale = 1.0 / math.sqrt(LX * LY * extent_z)
    contract = (((0, 1, 3, 4), (0, 1, 3, 4)), ((), ()))

    def operator(pair):
        momentum, direction = pair
        angle = phase_angle(momentum, coord_x, coord_y, coord_z, extent_z)
        cosine = jnp.cos(angle)
        sine = jnp.sin(angle)
        chosen = lax.dynamic_index_in_dim(displaced, direction, 0, keepdims=False).astype(
            jnp.float32
        )
        phased_re = (cosine * chosen[0] + sine * chosen[1]).astype(jnp.bfloat16)
        phased_im = (cosine * chosen[1] - sine * chosen[0]).astype(jnp.bfloat16)
        real_part = lax.dot_general(
            smeared, jnp.stack([phased_re, phased_im]), contract, preferred_element_type=jnp.float32
        )
        imag_part = lax.dot_general(
            smeared,
            jnp.stack([phased_im, -phased_re]),
            contract,
            preferred_element_type=jnp.float32,
        )
        return jnp.concatenate([real_part, imag_part], axis=1) * scale

    partial_sum = lax.map(operator, (momenta, displacements))
    levels = blocks.bit_length() - 1
    base = TG.bit_length() - 1
    piece = partial_sum
    for level in range(levels):
        upper_bit = block >> level & 1
        half = piece.shape[1] // 2
        lower_half = piece[:, :half]
        upper_half = piece[:, half:]
        keep = jnp.where(upper_bit == 1, upper_half, lower_half)
        sending = jnp.where(upper_bit == 1, lower_half, upper_half)
        piece = keep + partner(sending, base + level)
    for level in reversed(range(levels)):
        upper_bit = block >> level & 1
        other = partner(piece, base + level)
        piece = jnp.where(
            upper_bit == 1,
            jnp.concatenate([other, piece], axis=1),
            jnp.concatenate([piece, other], axis=1),
        )
    elem = piece.astype(jnp.bfloat16)
    operators = elem.shape[0]
    spins = perambulators.shape[3] // vector_count
    left = elem.reshape(-1, 2 * vector_count)
    sandwich_list = []
    for neighbour_index in range(HOPS):
        perambulator_real = perambulators[neighbour_index, 0]
        perambulator_imaginary = perambulators[neighbour_index, 1]
        right = jnp.concatenate(
            [
                jnp.concatenate([perambulator_real, perambulator_imaginary], axis=1),
                jnp.concatenate([-perambulator_imaginary, perambulator_real], axis=1),
            ],
            axis=0,
        )
        product = jnp.dot(left, right, preferred_element_type=jnp.float32).astype(jnp.bfloat16)
        product = product.reshape(operators, vector_count, 2, spins, vector_count)
        tau_re3 = perambulator_real.reshape(vector_count, spins, vector_count)
        tau_im3 = perambulator_imaginary.reshape(vector_count, spins, vector_count)
        sandwich_real = jnp.einsum(
            "asp,masl->mspl", tau_re3, product[:, :, 0], preferred_element_type=jnp.float32
        )
        sandwich_real = sandwich_real + jnp.einsum(
            "asp,masl->mspl", tau_im3, product[:, :, 1], preferred_element_type=jnp.float32
        )
        sandwich_imaginary = jnp.einsum(
            "asp,masl->mspl", tau_re3, product[:, :, 1], preferred_element_type=jnp.float32
        )
        sandwich_imaginary = sandwich_imaginary - jnp.einsum(
            "asp,masl->mspl", tau_im3, product[:, :, 0], preferred_element_type=jnp.float32
        )
        sandwich_list.append((sandwich_real, sandwich_imaginary))
    arrived = elem
    results = []
    for neighbour_index in range(HOPS):
        arrived = passed_along(arrived, "space", 1)
        source_vector = arrived.astype(jnp.float32)
        sandwich_real, sandwich_imaginary = sandwich_list[neighbour_index]
        entry_value = jnp.sum(
            sandwich_real * source_vector[:, None, :, :vector_count], axis=(2, 3)
        ) + jnp.sum(sandwich_imaginary * source_vector[:, None, :, vector_count:], axis=(2, 3))
        results.append(entry_value)
    return (smeared.reshape(2, 3, vector_count, depth * plane), jnp.stack(results))


def solution(mesh):
    placed = (
        P(None, None, None, ("cfg", "space")),
        P(None, None, None, None, ("cfg", "space")),
        P(),
        P(),
        P(None, None, None, ("cfg", "space")),
    )
    return jax.shard_map(
        body,
        mesh=mesh,
        in_specs=placed,
        out_specs=(P(None, None, None, ("cfg", "space")), P(None, None, ("cfg", "space"))),
        check_vma=False,
    )
```

profile of v0, /device:TPU:0, one launch (start us, length us, event | category | flops | bytes accessed | tf_op | source)
XLA Modules:
  0.0 452.6 jit_solution(8483772226990471881)
XLA Ops:
  2.6 4.1 collective-permute-start
  12.2 29.5 %collective-permute-done.1 = bf16[768,256]{1,0:T(8,128)(2,1)S(1)} collective-permute-done((bf16[768,256]{1,0:T(8,128)(2,1)S(1)}, bf16[768,256]{1,0:T(8,128)(2,1)S(1)}, u32[]{:S(2)}, u32[]{:S(2)}) %collective-permute-start.1) | collective-permute-done | bytes 393248 | tf_op jit(solution)/shard_map/ppermute | solution.py:19
  57.2 2.1 add_bitcast_fusion.37
  76.5 2.9 collective-permute-start.3
  81.5 31.3 %collective-permute-done.3 = bf16[768,256]{1,0:T(8,128)(2,1)S(1)} collective-permute-done((bf16[768,256]{1,0:T(8,128)(2,1)}, bf16[768,256]{1,0:T(8,128)(2,1)S(1)}, u32[]{:S(2)}, u32[]{:S(2)}) %collective-permute-start.3) | collective-permute-done | bytes 393248 | tf_op jit(solution)/shard_map/ppermute | solution.py:19
  123.9 2.2 add_bitcast_fusion.16
  151.1 16.5 %collective-permute-done.4 = bf16[768,256]{1,0:T(8,128)(2,1)S(1)} collective-permute-done((bf16[768,256]{1,0:T(8,128)(2,1)S(1)}, bf16[768,256]{1,0:T(8,128)(2,1)S(1)}, u32[]{:S(2)}, u32[]{:S(2)}) %collective-permute-start.4) | collective-permute-done | bytes 393248 | tf_op jit(solution)/shard_map/ppermute | solution.py:19
  167.9 2.2 pad_maximum_fusion
  188.1 80.1 %while.14 = (s32[]{:T(128)}, f32[8,128,256]{2,1,0:T(8,128)}, s32[8,3]{0,1:T(4,128)S(1)}, s32[8]{0:T(128)}, bf16[3,2,3,128,2,256]{3,5,4,2,1,0:T(8,128)(2,1)S(1)},...) while((s32[]{:T(128)}, f32[8,128,256]{2,1,0:T(8,128)}, ...), condition=%wide.region_1.2_spmd.clone, body=%wide.region_0.1_spmd.clone.sunk | while | flops 204363264 | bytes 35935700 | solution.py:193
  268.3 2.2 slice_select_fusion
  278.0 17.3 %collective-permute-done.5 = f32[8,64,256]{2,1,0:T(8,128)} collective-permute-done((f32[8,64,256]{2,1,0:T(8,128)}, f32[8,64,256]{2,1,0:T(8,128)}, u32[]{:S(2)}, u32[]{:S(2)}) %collective-permute-start.5) | collective-permute-done | bytes 524320 | tf_op jit(solution)/shard_map/ppermute | solution.py:23
  299.2 12.7 %collective-permute-done.6 = bf16[8,64,256]{2,1,0:T(8,128)(2,1)S(1)} collective-permute-done((bf16[8,64,256]{2,1,0:T(8,128)(2,1)}, bf16[8,64,256]{2,1,0:T(8,128)(2,1)S(1)}, u32[]{:S(2)}, u32[]{:S(2)}) %collective-permute-start.6) | collective-permute-done | bytes 262176 | tf_op jit(solution)/shard_map/ppermute | solution.py:23
  314.0 2.3 convert_bitcast_fusion.3
  317.7 3.1 fusion.222
  320.8 3.5 copy.365
  324.3 4.7 %copy.366 = bf16[8,128,1,8,128]{1,4,0,3,2:T(8,128)(2,1)} copy(bf16[8,128,1,8,128]{4,3,2,1,0:T(8,128)(2,1)} %get-tuple-element.318) | data formatting | bytes 4194304
  329.0 2.7 fusion.60
  331.7 2.7 fusion.58
  334.4 2.3 convert_bitcast_fusion.2
  338.1 3.1 fusion.223
  341.2 3.3 copy.369
  344.5 4.7 %copy.370 = bf16[8,128,1,8,128]{1,4,0,3,2:T(8,128)(2,1)} copy(bf16[8,128,1,8,128]{4,3,2,1,0:T(8,128)(2,1)} %get-tuple-element.320) | data formatting | bytes 4194304
  349.2 2.8 fusion.52
  352.0 2.7 fusion.50
  354.7 2.3 convert_bitcast_fusion.1
  358.5 3.1 fusion.224
  361.6 3.3 copy.373
  364.9 4.9 %copy.374 = bf16[8,128,1,8,128]{1,4,0,3,2:T(8,128)(2,1)} copy(bf16[8,128,1,8,128]{4,3,2,1,0:T(8,128)(2,1)} %get-tuple-element.322) | data formatting | bytes 4194304
  369.8 2.8 fusion.44
  372.6 2.7 fusion.42
  375.3 2.3 convert_bitcast_fusion
  379.0 3.1 fusion.225
  382.2 3.3 copy.377
  385.5 2.8 fusion.36
  388.2 4.1 copy.378
  392.3 4.3 fusion.34
  396.7 2.1 fusion.252
  401.0 3.6 fusion.30
  405.9 3.6 fusion.31
  409.6 2.2 collective-permute-done.8
  415.2 3.6 fusion.28
  420.0 3.6 fusion.29
  423.7 3.0 collective-permute-done.9
  426.8 2.1 fusion.254
  430.5 3.6 fusion.26
  435.4 3.6 fusion.27
  439.1 3.0 collective-permute-done.10
  446.3 3.9 fusion.24
  (1039 shorter events, 192.6 us)
Async XLA Ops:
  2.2 4.9 %copy-start.9 = (bf16[2,3,128,512]{2,3,1,0:T(8,128)(2,1)}, bf16[2,3,128,512]{2,3,1,0:T(8,128)(2,1)S(1)}, u32[]{:S(2)}) copy-start(bf16[2,3,128,512]{2,3,1,0:T(8,128)(2,1)S(1)} %copy.246) | copy-start | bytes 2359300
  2.6 39.3 %collective-permute-start = (bf16[786,256]{1,0:T(8,128)(2,1)S(1)}, bf16[786,256]{1,0:T(8,128)(2,1)S(1)}, u32[]{:S(2)}, u32[]{:S(2)}) collective-permute-start(bf16[786,256]{1,0:T(8,128)(2,1)S(1)} %pad_maximum_fusion.5), channel_id=1, source_target_pairs={{0,8},{1,9},{2,10},{3,11},{4,12},{5,13},{6,14},{7,15},{8,0},{9,1},... | collective-permute-start | bytes 1207304 | tf_op jit(solution)/shard_map/ppermute | solution.py:19
  6.9 34.7 %collective-permute-start.1 = (bf16[768,256]{1,0:T(8,128)(2,1)S(1)}, bf16[768,256]{1,0:T(8,128)(2,1)S(1)}, u32[]{:S(2)}, u32[]{:S(2)}) collective-permute-start(bf16[768,256]{1,0:T(8,128)(2,1)S(1)} %bitcast.791), channel_id=1, source_target_pairs={{0,8},{1,9},{2,10},{3,11},{4,12},{5,13},{6,14},{7,15},{8,0},{9,1},... | collective-permute-start | bytes 1179656 | tf_op jit(solution)/shard_map/ppermute | solution.py:19
  7.1 34.8 %copy-start.315 = (pred[256]{0:T(512)(128)(4,1)}, pred[256]{0:T(512)(128)(4,1)S(1)}, u32[]{:S(2)}) copy-start(pred[256]{0:T(512)(128)(4,1)S(1)} %broadcast_compare_fusion.1) | copy-start | bytes 772
  55.1 4.3 copy-start.297
  55.1 4.3 copy-start.299
  55.1 4.3 copy-start.301
  55.1 4.3 copy-start.303
  55.1 4.3 copy-start.305
  55.1 4.3 copy-start.307
  72.8 6.6 %copy-start.32 = (bf16[4,2,128,1024]{3,2,1,0:T(8,128)(2,1)S(1)}, bf16[4,2,128,1024]{3,2,1,0:T(8,128)(2,1)}, u32[]{:S(2)}) copy-start(bf16[4,2,128,1024]{3,2,1,0:T(8,128)(2,1)} %param.11) | copy-start | bytes 6291460
  75.6 38.1 %collective-permute-start.2 = (bf16[786,256]{1,0:T(8,128)(2,1)}, bf16[786,256]{1,0:T(8,128)(2,1)}, u32[]{:S(2)}, u32[]{:S(2)}) collective-permute-start(bf16[786,256]{1,0:T(8,128)(2,1)} %pad_maximum_fusion.4), channel_id=1, source_target_pairs={{0,8},{1,9},{2,10},{3,11},{4,12},{5,13},{6,14},{7,15},{8,0},{9,1},... | collective-permute-start | bytes 1207304 | tf_op jit(solution)/shard_map/ppermute | solution.py:19
  76.5 36.3 %collective-permute-start.3 = (bf16[768,256]{1,0:T(8,128)(2,1)}, bf16[768,256]{1,0:T(8,128)(2,1)S(1)}, u32[]{:S(2)}, u32[]{:S(2)}) collective-permute-start(bf16[768,256]{1,0:T(8,128)(2,1)} %bitcast.156), channel_id=1, source_target_pairs={{0,8},{1,9},{2,10},{3,11},{4,12},{5,13},{6,14},{7,15},{8,0},{9,1},... | collective-permute-start | bytes 1179656 | tf_op jit(solution)/shard_map/ppermute | solution.py:19
  122.6 3.5 copy-start.130
  122.6 3.5 copy-start.133
  122.6 3.5 copy-start.136
  148.8 18.8 %collective-permute-start.4 = (bf16[768,256]{1,0:T(8,128)(2,1)S(1)}, bf16[768,256]{1,0:T(8,128)(2,1)S(1)}, u32[]{:S(2)}, u32[]{:S(2)}) collective-permute-start(bf16[768,256]{1,0:T(8,128)(2,1)S(1)} %bitcast.794), channel_id=1, source_target_pairs={{0,8},{1,9},{2,10},{3,11},{4,12},{5,13},{6,14},{7,15},{8,0},{9,1},... | collective-permute-start | bytes 1179656 | tf_op jit(solution)/shard_map/ppermute | solution.py:19
  188.1 6.7 %copy-start.6 = (bf16[3,2,3,128,2,256]{3,5,4,2,1,0:T(8,128)(2,1)}, bf16[3,2,3,128,2,256]{3,5,4,2,1,0:T(8,128)(2,1)S(1)}, u32[]{:S(2)}) copy-start(bf16[3,2,3,128,2,256]{3,5,4,2,1,0:T(8,128)(2,1)S(1)} %get-tuple-element.846) | copy-start | bytes 7077892 | tf_op jit(solution)/shard_map/while
  198.2 6.7 %copy-start.6 = (bf16[3,2,3,128,2,256]{3,5,4,2,1,0:T(8,128)(2,1)}, bf16[3,2,3,128,2,256]{3,5,4,2,1,0:T(8,128)(2,1)S(1)}, u32[]{:S(2)}) copy-start(bf16[3,2,3,128,2,256]{3,5,4,2,1,0:T(8,128)(2,1)S(1)} %get-tuple-element.846) | copy-start | bytes 7077892 | tf_op jit(solution)/shard_map/while
  208.2 6.7 %copy-start.6 = (bf16[3,2,3,128,2,256]{3,5,4,2,1,0:T(8,128)(2,1)}, bf16[3,2,3,128,2,256]{3,5,4,2,1,0:T(8,128)(2,1)S(1)}, u32[]{:S(2)}) copy-start(bf16[3,2,3,128,2,256]{3,5,4,2,1,0:T(8,128)(2,1)S(1)} %get-tuple-element.846) | copy-start | bytes 7077892 | tf_op jit(solution)/shard_map/while
  218.2 6.7 %copy-start.6 = (bf16[3,2,3,128,2,256]{3,5,4,2,1,0:T(8,128)(2,1)}, bf16[3,2,3,128,2,256]{3,5,4,2,1,0:T(8,128)(2,1)S(1)}, u32[]{:S(2)}) copy-start(bf16[3,2,3,128,2,256]{3,5,4,2,1,0:T(8,128)(2,1)S(1)} %get-tuple-element.846) | copy-start | bytes 7077892 | tf_op jit(solution)/shard_map/while
  228.2 6.7 %copy-start.6 = (bf16[3,2,3,128,2,256]{3,5,4,2,1,0:T(8,128)(2,1)}, bf16[3,2,3,128,2,256]{3,5,4,2,1,0:T(8,128)(2,1)S(1)}, u32[]{:S(2)}) copy-start(bf16[3,2,3,128,2,256]{3,5,4,2,1,0:T(8,128)(2,1)S(1)} %get-tuple-element.846) | copy-start | bytes 7077892 | tf_op jit(solution)/shard_map/while
  238.2 6.7 %copy-start.6 = (bf16[3,2,3,128,2,256]{3,5,4,2,1,0:T(8,128)(2,1)}, bf16[3,2,3,128,2,256]{3,5,4,2,1,0:T(8,128)(2,1)S(1)}, u32[]{:S(2)}) copy-start(bf16[3,2,3,128,2,256]{3,5,4,2,1,0:T(8,128)(2,1)S(1)} %get-tuple-element.846) | copy-start | bytes 7077892 | tf_op jit(solution)/shard_map/while
  248.2 6.7 %copy-start.6 = (bf16[3,2,3,128,2,256]{3,5,4,2,1,0:T(8,128)(2,1)}, bf16[3,2,3,128,2,256]{3,5,4,2,1,0:T(8,128)(2,1)S(1)}, u32[]{:S(2)}) copy-start(bf16[3,2,3,128,2,256]{3,5,4,2,1,0:T(8,128)(2,1)S(1)} %get-tuple-element.846) | copy-start | bytes 7077892 | tf_op jit(solution)/shard_map/while
  258.2 6.7 %copy-start.6 = (bf16[3,2,3,128,2,256]{3,5,4,2,1,0:T(8,128)(2,1)}, bf16[3,2,3,128,2,256]{3,5,4,2,1,0:T(8,128)(2,1)S(1)}, u32[]{:S(2)}) copy-start(bf16[3,2,3,128,2,256]{3,5,4,2,1,0:T(8,128)(2,1)S(1)} %get-tuple-element.846) | copy-start | bytes 7077892 | tf_op jit(solution)/shard_map/while
  268.3 3.9 copy-start.44
  268.3 5.4 %copy-start.43 = (bf16[1,1,128,1024]{3,2,1,0:T(8,128)(2,1)S(1)}, bf16[1,1,128,1024]{3,2,1,0:T(8,128)(2,1)}, u32[]{:S(2)}) copy-start(bf16[1,1,128,1024]{3,2,1,0:T(8,128)(2,1)} %get-tuple-element.359) | copy-start | bytes 786436
  268.3 6.2 %copy-start.42 = (bf16[1,1,128,1024]{3,2,1,0:T(8,128)(2,1)S(1)}, bf16[1,1,128,1024]{3,2,1,0:T(8,128)(2,1)}, u32[]{:S(2)}) copy-start(bf16[1,1,128,1024]{3,2,1,0:T(8,128)(2,1)} %get-tuple-element.356) | copy-start | bytes 786436
  268.3 6.4 %copy-start.41 = (bf16[1,1,128,1024]{3,2,1,0:T(8,128)(2,1)S(1)}, bf16[1,1,128,1024]{3,2,1,0:T(8,128)(2,1)}, u32[]{:S(2)}) copy-start(bf16[1,1,128,1024]{3,2,1,0:T(8,128)(2,1)} %get-tuple-element.357) | copy-start | bytes 786436
  268.3 7.2 %copy-start.40 = (bf16[1,1,128,1024]{3,2,1,0:T(8,128)(2,1)S(1)}, bf16[1,1,128,1024]{3,2,1,0:T(8,128)(2,1)}, u32[]{:S(2)}) copy-start(bf16[1,1,128,1024]{3,2,1,0:T(8,128)(2,1)} %get-tuple-element.361) | copy-start | bytes 786436
  270.5 5.2 %copy-start.39 = (bf16[1,1,128,1024]{3,2,1,0:T(8,128)(2,1)S(1)}, bf16[1,1,128,1024]{3,2,1,0:T(8,128)(2,1)}, u32[]{:S(2)}) copy-start(bf16[1,1,128,1024]{3,2,1,0:T(8,128)(2,1)} %get-tuple-element.355) | copy-start | bytes 786436
  270.5 24.8 %collective-permute-start.5 = (f32[8,64,256]{2,1,0:T(8,128)}, f32[8,64,256]{2,1,0:T(8,128)}, u32[]{:S(2)}, u32[]{:S(2)}) collective-permute-start(f32[8,64,256]{2,1,0:T(8,128)} %slice_select_fusion), channel_id=1, source_target_pairs={{0,8},{1,9},{2,10},{3,11},{4,12},{5,13},{6,14},{7,15},{8,0},{9,1},... | collective-permute-start | bytes 1572872 | tf_op jit(solution)/shard_map/ppermute | solution.py:23
  272.4 41.6 %copy-start.30 = (bf16[1,1,128,1024]{2,3,1,0:T(8,128)(2,1)}, bf16[1,1,128,1024]{2,3,1,0:T(8,128)(2,1)S(1)}, u32[]{:S(2)}) copy-start(bf16[1,1,128,1024]{2,3,1,0:T(8,128)(2,1)S(1)} %copy.363) | copy-start | bytes 786436
  272.4 22.9 %copy-start.13 = (f32[8,128,256]{2,1,0:T(8,128)S(1)}, f32[8,128,256]{2,1,0:T(8,128)}, u32[]{:S(2)}) copy-start(f32[8,128,256]{2,1,0:T(8,128)} %get-tuple-element.867) | copy-start | bytes 3145732
  276.5 21.5 %copy-start.11 = (bf16[1,3,128,2,256]{2,4,3,1,0:T(8,128)(2,1)S(1)}, bf16[1,3,128,2,256]{2,4,3,1,0:T(8,128)(2,1)}, u32[]{:S(2)}) copy-start(bf16[1,3,128,2,256]{2,4,3,1,0:T(8,128)(2,1)} %copy-done.10) | copy-start | bytes 1179652
  297.2 14.8 %collective-permute-start.6 = (bf16[8,64,256]{2,1,0:T(8,128)(2,1)}, bf16[8,64,256]{2,1,0:T(8,128)(2,1)S(1)}, u32[]{:S(2)}, u32[]{:S(2)}) collective-permute-start(bf16[8,64,256]{2,1,0:T(8,128)(2,1)} %select_add_fusion), channel_id=1, source_target_pairs={{0,8},{1,9},{2,10},{3,11},{4,12},{5,13},{6,14},{7,15},{8,0},{9,1},... | collective-permute-start | bytes 786440 | tf_op jit(solution)/shard_map/ppermute | solution.py:23
  297.9 16.1 %copy-start.12 = (bf16[1,1,128,1024]{2,3,1,0:T(8,128)(2,1)S(1)}, bf16[1,1,128,1024]{2,3,1,0:T(8,128)(2,1)}, u32[]{:S(2)}) copy-start(bf16[1,1,128,1024]{2,3,1,0:T(8,128)(2,1)} %copy.364) | copy-start | bytes 786436
  297.9 16.1 %copy-start.87 = (bf16[128,1024]{0,1:T(8,128)(2,1)S(1)}, bf16[128,1024]{0,1:T(8,128)(2,1)}, u32[]{:S(2)}) copy-start(bf16[128,1024]{0,1:T(8,128)(2,1)} %bitcast_negate_fusion.3) | copy-start | bytes 786436
  313.9 82.7 %collective-permute-start.7 = (bf16[8,128,256]{2,1,0:T(8,128)(2,1)}, bf16[8,128,256]{2,1,0:T(8,128)(2,1)}, u32[]{:S(2)}, u32[]{:S(2)}) collective-permute-start(bf16[8,128,256]{2,1,0:T(8,128)(2,1)} %fusion.64), channel_id=1, source_target_pairs={{0,1},{1,2},{2,3},{3,4},{4,5},{5,6},{6,7},{7,8},{8,9},{9,10},{10,1... | collective-permute-start | bytes 1572872 | tf_op jit(solution)/shard_map/ppermute | solution.py:19
  324.3 4.7 %copy-start.4 = (bf16[8,128,1,8,128]{1,4,0,3,2:T(8,128)(2,1)}, bf16[8,128,1,8,128]{1,4,0,3,2:T(8,128)(2,1)S(1)}, u32[]{:S(2)}) copy-start(bf16[8,128,1,8,128]{1,4,0,3,2:T(8,128)(2,1)S(1)} %copy.365) | copy-start | bytes 6291460
  344.5 4.7 %copy-start.2 = (bf16[8,128,1,8,128]{1,4,0,3,2:T(8,128)(2,1)}, bf16[8,128,1,8,128]{1,4,0,3,2:T(8,128)(2,1)S(1)}, u32[]{:S(2)}) copy-start(bf16[8,128,1,8,128]{1,4,0,3,2:T(8,128)(2,1)S(1)} %copy.369) | copy-start | bytes 6291460
  364.8 5.0 %copy-start = (bf16[8,128,1,8,128]{1,4,0,3,2:T(8,128)(2,1)}, bf16[8,128,1,8,128]{1,4,0,3,2:T(8,128)(2,1)S(1)}, u32[]{:S(2)}) copy-start(bf16[8,128,1,8,128]{1,4,0,3,2:T(8,128)(2,1)S(1)} %copy.373) | copy-start | bytes 6291460
  396.7 4.3 copy-start.31
  400.1 11.7 %collective-permute-start.8 = (bf16[8,128,256]{2,1,0:T(8,128)(2,1)}, bf16[8,128,256]{2,1,0:T(8,128)(2,1)}, u32[]{:S(2)}, u32[]{:S(2)}) collective-permute-start(bf16[8,128,256]{2,1,0:T(8,128)(2,1)} %collective-permute-done.7), channel_id=1, source_target_pairs={{0,1},{1,2},{2,3},{3,4},{4,5},{5,6},{6,7},{7,8},{8,9},{9,10},{10,1... | collective-permute-start | bytes 1572872 | tf_op jit(solution)/shard_map/ppermute | solution.py:19
  409.5 5.7 %copy-start.29 = (bf16[1,1,128,1024]{2,3,1,0:T(8,128)(2,1)S(1)}, bf16[1,1,128,1024]{2,3,1,0:T(8,128)(2,1)}, u32[]{:S(2)}) copy-start(bf16[1,1,128,1024]{2,3,1,0:T(8,128)(2,1)} %copy.367) | copy-start | bytes 786436
  415.1 11.7 %collective-permute-start.9 = (bf16[8,128,256]{2,1,0:T(8,128)(2,1)}, bf16[8,128,256]{2,1,0:T(8,128)(2,1)}, u32[]{:S(2)}, u32[]{:S(2)}) collective-permute-start(bf16[8,128,256]{2,1,0:T(8,128)(2,1)} %collective-permute-done.8), channel_id=1, source_target_pairs={{0,1},{1,2},{2,3},{3,4},{4,5},{5,6},{6,7},{7,8},{8,9},{9,10},{10,1... | collective-permute-start | bytes 1572872 | tf_op jit(solution)/shard_map/ppermute | solution.py:19
  430.1 12.0 %collective-permute-start.10 = (bf16[8,128,256]{2,1,0:T(8,128)(2,1)}, bf16[8,128,256]{2,1,0:T(8,128)(2,1)}, u32[]{:S(2)}, u32[]{:S(2)}) collective-permute-start(bf16[8,128,256]{2,1,0:T(8,128)(2,1)} %collective-permute-done.9), channel_id=1, source_target_pairs={{0,1},{1,2},{2,3},{3,4},{4,5},{5,6},{6,7},{7,8},{8,9},{9,10},{10,1... | collective-permute-start | bytes 1572872 | tf_op jit(solution)/shard_map/ppermute | solution.py:19
  446.3 4.2 copy-start.8
  (312 other events, 554.0 us)
where the time goes:
time: 460 us; the launch traced here: 453 us
  local copies, waits for them, and re-layouts  139 us (30%)
  waiting for transfers between devices  116 us (25%)
  other arithmetic  102 us (22%)
  matrix products  65 us (14%)
  loops' own time  16.4 us (4%)
  starting transfers between devices  8.58 us (2%)
  between operations  5.65 us (1%)
    ppermute x9, waiting for transfers between devices, passed_along(): lax.ppermute(shard, axis, [(i, (i + by) % peers) for i in range(peers)])  85.5 us
    unnamed x656, local copies, waits for them, and re-layouts  55.3 us
    ppermute x2, waiting for transfers between devices, partner_2(): lax.ppermute(shard, axis, [(i, i ^ 1 << apart) for i in range(lax.axis_si...  30 us
    another operation x24, other arithmetic, link_apply(): return (jnp.stack(outs_re), jnp.stack(outs_im))  26.1 us
    cos x8, other arithmetic, operator(): cosine = jnp.cos(angle)  16.8 us
    another operation x1, loops' own time, body(): partial_sum = lax.map(operator, (momenta, displacements))  16.4 us
    dot_general x4, matrix products, body(): jnp.einsum('asp,masl->mspl', tau_re3, product[:, :, 1], preferred_element...  14.7 us
    another operation x13, other arithmetic  13 us
  transfers between devices with their start and end apart: 11, of which 8 were waited for; matrix products, arithmetic and copies ran while one was open for 29% of the time, Pallas kernels for 0%

commit v1 on v0

--- a/solution.py
+++ b/solution.py
@@ -1,8 +1,12 @@
+import functools
 import math
 
 import jax
 import jax.numpy as jnp
+import numpy as np
 from jax import lax
+from jax.experimental import pallas as pl
+from jax.experimental.pallas import tpu as pltpu
 from jax.sharding import PartitionSpec as P
 
 TG = 8
@@ -111,7 +115,7 @@
     return partner_2(values, "space", bit_place)
 
 
-def body(vectors, links, momenta, displacements, perambulators):
+def body_many(vectors, links, momenta, displacements, perambulators):
     vector_count = vectors.shape[2]
     plane = LX * LY
     depth = vectors.shape[3] // plane
@@ -255,6 +259,407 @@
     return (smeared.reshape(2, 3, vector_count, depth * plane), jnp.stack(results))
 
 
+COMPONENTS = 6
+SLOTS = 40
+WIDE = SLOTS * LX
+USED = 32 * LX
+MIB = 1 << 20
+VMEM = pl.BlockSpec(memory_space=pltpu.VMEM)
+SMEM = pl.BlockSpec(memory_space=pltpu.SMEM)
+
+
+def hop_slots():
+    slots = {}
+    for q in range(COMPONENTS):
+        slots[q] = ("xf", q)
+        slots[8 + q] = ("zf", q)
+        slots[16 + q] = ("yf", q)
+        slots[24 + q] = ("zb", q)
+        slots[32 + q] = ("xb", q)
+        slots[(6, 7, 14, 15, 22, 23)[q]] = ("yb", q)
+    return slots
+
+
+def stencil_constants():
+    pick = np.zeros((COMPONENTS, 80, WIDE), np.float32)
+    where = np.zeros((8, WIDE), np.int32)
+    near = np.zeros((LX, WIDE), np.float32)
+    for slot, (hop, q_in) in hop_slots().items():
+        lanes = slice(slot * LX, (slot + 1) * LX)
+        part_in, colour_in = divmod(q_in, 3)
+        axis = "xyz".index(hop[0])
+        columns = np.arange(LX)
+        where[0, lanes] = (columns - 1) % LX if hop == "xf" else columns
+        where[1, lanes] = 1 if hop == "yb" else 0
+        shift = {"xf": 1, "xb": -1}.get(hop, 0)
+        for x_out in range(LX):
+            near[x_out, slot * LX + (x_out + shift) % LX] = 1.0
+        for q_out in range(COMPONENTS):
+            part_out, colour_out = divmod(q_out, 3)
+            mixed = int(part_in != part_out)
+            if hop[1] == "f":
+                a, b = colour_out, colour_in
+                sign = -1.0 if (part_out, part_in) == (0, 1) else 1.0
+            else:
+                a, b = colour_in, colour_out
+                sign = -1.0 if (part_out, part_in) == (1, 0) else 1.0
+            row = ((axis * 2 + mixed) * 3 + a) * 3 + b
+            if hop == "zb":
+                row = 54 + (mixed * 3 + a) * 3 + b
+            pick[q_out, row, lanes] = sign
+    return pick, where, near
+
+
+def stencil_kernel(links_ref, pick_ref, where_ref, near_ref, full_ref, ahead_ref):
+    planes = links_ref.shape[0]
+    plane = links_ref.shape[2]
+    ones = jnp.ones((LX, 80), jnp.bfloat16)
+
+    def one_row(y, carry):
+        row = y - where_ref[1:2, :]
+        row = jnp.where(row < 0, row + LY, row)
+        source = row * LX + where_ref[0:1, :]
+        spread = (
+            lax.broadcasted_iota(jnp.int32, (plane, WIDE), 0) == jnp.broadcast_to(source, (plane, WIDE))
+        )
+        spread = jnp.where(spread, 1.0, 0.0).astype(jnp.bfloat16)
+        for z in range(planes):
+            laid = jnp.dot(links_ref[z], spread, preferred_element_type=jnp.float32).astype(jnp.bfloat16)
+            for q in range(COMPONENTS):
+                line = jnp.dot(ones, laid * pick_ref[q], preferred_element_type=jnp.float32)
+                line = line * near_ref[...]
+                rows = slice(q * LX, (q + 1) * LX)
+                first = line[:, : 8 * LX]
+                ahead_ref[z * LY + y, rows, :] = first.astype(jnp.bfloat16)
+                full_ref[z * LY + y, rows, : 8 * LX] = (first + line[:, USED:]).astype(jnp.bfloat16)
+                full_ref[z * LY + y, rows, 8 * LX :] = line[:, 8 * LX : USED].astype(jnp.bfloat16)
+        return carry
+
+    lax.fori_loop(0, LY, one_row, 0)
+
+
+def smear_kernel(
+    own_ref, other_ref, full_ref, ahead_ref, smeared_ref, wide_ref, moved_ref, start, first, last
+):
+    rows = full_ref.shape[0]
+    planes = rows // LY
+    half = own_ref.shape[1]
+    sites = rows * LX
+    vector_count = own_ref.shape[3]
+    start[:, :half] = own_ref[...]
+    start[:, half:] = other_ref[...]
+    zero = jnp.zeros((LX, vector_count), jnp.bfloat16)
+    slots = hop_slots()
+
+    def places(z, y):
+        up = jnp.where(y == LY - 1, 0, y + 1)
+        down = jnp.where(y == 0, LY - 1, y - 1)
+        above = (z + 1) % planes
+        below = (z - 1) % planes
+        return {
+            "xf": z * LY + y,
+            "yf": z * LY + up,
+            "yb": z * LY + down,
+            "zf": above * LY + y,
+            "zb": below * LY + y,
+        }
+
+    def gathered(ref, place, wanted, hops):
+        pieces = []
+        for slot in wanted:
+            hop, q = slots.get(slot, (None, 0))
+            pieces.append(ref[q, place[hop]] if hop in hops else zero)
+        return jnp.concatenate(pieces, axis=0)
+
+    def sweep(source, target):
+        def one_row(y, carry):
+            for z in range(planes):
+                place = places(z, y)
+                r = z * LY + y
+                around = gathered(source, place, range(32), ("xf", "yf", "yb", "zf", "zb"))
+                total = jnp.dot(full_ref[r], around, preferred_element_type=jnp.float32)
+                for q in range(COMPONENTS):
+                    value = (1.0 - 6.0 * KAPPA) * source[q, r].astype(jnp.float32)
+                    value = value + KAPPA * total[q * LX : (q + 1) * LX]
+                    target[q, r] = value.astype(jnp.bfloat16)
+            return carry
+
+        lax.fori_loop(0, LY, one_row, 0)
+
+    sweep(start, first)
+    sweep(first, last)
+
+    def displace(y, carry):
+        for z in range(planes):
+            place = places(z, y)
+            r = z * LY + y
+            for axis, (hop, begin) in enumerate((("xf", 0), ("yf", 16), ("zf", 8))):
+                around = gathered(last, place, range(begin, begin + 8), (hop,))
+                if axis == 0:
+                    matrix = ahead_ref[r]
+                else:
+                    matrix = full_ref[r, :, begin * LX : (begin + 8) * LX]
+                total = jnp.dot(matrix, around, preferred_element_type=jnp.float32)
+                for q in range(COMPONENTS):
+                    moved_ref[axis, q, r] = total[q * LX : (q + 1) * LX].astype(jnp.bfloat16)
+        return carry
+
+    lax.fori_loop(0, LY, displace, 0)
+    for q in range(COMPONENTS):
+        for b in range(sites // 128):
+            tile = last[q, b * 8 : (b + 1) * 8].reshape(128, vector_count)
+            tile = jnp.transpose(tile)
+            wide_ref[:, q * sites + b * 128 : q * sites + (b + 1) * 128] = tile
+            if b * 8 < half:
+                smeared_ref[q, :, b * 128 : (b + 1) * 128] = tile
+
+
+def elemental_kernel(
+    offset, scale, direction_ref, row_cos_ref, row_sin_ref, cos_ref, sin_ref, wide_ref, moved_ref, out_ref, phased
+):
+    rows = moved_ref.shape[2]
+    sites = rows * LX
+    vector_count = moved_ref.shape[4]
+    for index in range(out_ref.shape[0]):
+        m = offset + index
+        direction = direction_ref[m]
+        base_cos = cos_ref[m]
+        base_sin = sin_ref[m]
+
+        def one_row(r, carry):
+            turn_cos = row_cos_ref[m, r]
+            turn_sin = row_sin_ref[m, r]
+            cosine = base_cos * turn_cos - base_sin * turn_sin
+            sine = base_sin * turn_cos + base_cos * turn_sin
+            for c in range(3):
+                real = moved_ref[direction, c, r].astype(jnp.float32)
+                imag = moved_ref[direction, 3 + c, r].astype(jnp.float32)
+                phased_re = cosine * real + sine * imag
+                phased_im = cosine * imag - sine * real
+                upper = pl.ds(pl.multiple_of(c * sites + r * LX, LX), LX)
+                lower = pl.ds(pl.multiple_of((3 + c) * sites + r * LX, LX), LX)
+                phased[index % 2, upper, :vector_count] = phased_re.astype(jnp.bfloat16)
+                phased[index % 2, upper, vector_count:] = phased_im.astype(jnp.bfloat16)
+                phased[index % 2, lower, :vector_count] = phased_im.astype(jnp.bfloat16)
+                phased[index % 2, lower, vector_count:] = (-phased_re).astype(jnp.bfloat16)
+            return carry
+
+        lax.fori_loop(0, rows, one_row, 0, unroll=4)
+        total = jnp.dot(wide_ref[...], phased[index % 2], preferred_element_type=jnp.float32)
+        out_ref[index] = (total * scale).astype(jnp.bfloat16)
+
+
+def right_kernel(elem_ref, tau_ref, out_ref):
+    operators, vector_count, wide = elem_ref.shape
+    left = elem_ref[...].reshape(operators * vector_count, wide)
+    spins = tau_ref.shape[3] // vector_count
+    for s in range(spins):
+        lanes = slice(s * vector_count, (s + 1) * vector_count)
+        real = tau_ref[0, 0, :, lanes]
+        imag = tau_ref[0, 1, :, lanes]
+        right = jnp.concatenate(
+            [jnp.concatenate([real, imag], axis=1), jnp.concatenate([-imag, real], axis=1)], axis=0
+        )
+        out_ref[0, s] = jnp.dot(left, right, preferred_element_type=jnp.float32).astype(jnp.bfloat16)
+
+
+def trace_kernel(which_ref, source_ref, tau_ref, product_ref, out_ref):
+    operators, vector_count, wide = source_ref.shape[1:]
+    spins = tau_ref.shape[3] // vector_count
+    left = jnp.concatenate(
+        [
+            jnp.concatenate(
+                [
+                    tau_ref[0, part, :, s * vector_count : (s + 1) * vector_count]
+                    for part in range(2)
+                ],
+                axis=1,
+            )
+            for s in range(spins)
+        ],
+        axis=0,
+    )
+
+    def one_operator(m, carry):
+        top = source_ref[0, m]
+        bottom = jnp.concatenate([-top[:, vector_count:], top[:, :vector_count]], axis=1)
+        right = jnp.concatenate([top, bottom], axis=0)
+        other = jnp.dot(left, right, preferred_element_type=jnp.float32)
+        lines = []
+        for s in range(spins):
+            rows = pl.ds(pl.multiple_of(m * vector_count, vector_count), vector_count)
+            mine = product_ref[0, s, rows, :].astype(jnp.float32)
+            both = mine * other[s * vector_count : (s + 1) * vector_count]
+            both = jnp.sum(both.reshape(vector_count // 8, 8, wide), axis=0)
+            both = both[:, :vector_count] + both[:, vector_count:]
+            lines.append(jnp.sum(both, axis=0, keepdims=True))
+        out_ref[0, m] = jnp.concatenate(lines, axis=0)
+        return carry
+
+    lax.fori_loop(0, operators, one_operator, 0)
+
+
+def swapped(values, bit):
+    return partner_2(values, "space", bit)
+
+
+def correlators(elem, perambulators):
+    operators, vector_count, wide = elem.shape
+    spins = perambulators.shape[3] // vector_count
+    index = lax.axis_index("space")
+    core = index & 1
+    column = index >> 1 & 1
+    back_4 = swapped(elem, 2)
+    back_2 = swapped(jnp.where(column == 0, elem, back_4), 1)
+    early = swapped(jnp.where(core == 0, elem, back_4), 0)
+    late = swapped(back_2, 0)
+    tau_spec = pl.BlockSpec((1, 2, vector_count, spins * vector_count), lambda h: (h, 0, 0, 0))
+    products = pl.pallas_call(
+        right_kernel,
+        grid=(HOPS,),
+        in_specs=[pl.BlockSpec((operators, vector_count, wide), lambda h: (0, 0, 0)), tau_spec],
+        out_specs=pl.BlockSpec((1, spins, operators * vector_count, wide), lambda h: (h, 0, 0, 0)),
+        out_shape=jax.ShapeDtypeStruct((HOPS, spins, operators * vector_count, wide), jnp.bfloat16),
+        compiler_params=pltpu.CompilerParams(vmem_limit_bytes=40 * MIB),
+        cost_estimate=pl.CostEstimate(flops=4_300_000_000, bytes_accessed=20_000_000, transcendentals=0),
+        name="right",
+    )(elem, perambulators)
+
+    def traces(sources, hops):
+        count = len(sources)
+        which = jnp.stack([jnp.int32(h) for h in hops])
+        stacked = jnp.stack(sources)
+        return pl.pallas_call(
+            trace_kernel,
+            grid_spec=pltpu.PrefetchScalarGridSpec(
+                num_scalar_prefetch=1,
+                grid=(count,),
+                in_specs=[
+                    pl.BlockSpec((1, operators, vector_count, wide), lambda g, w: (g, 0, 0, 0)),
+                    pl.BlockSpec((1, 2, vector_count, spins * vector_count), lambda g, w: (w[g], 0, 0, 0)),
+                    pl.BlockSpec((1, spins, operators * vector_count, wide), lambda g, w: (w[g], 0, 0, 0)),
+                ],
+                out_specs=pl.BlockSpec((1, operators, spins, vector_count), lambda g, w: (g, 0, 0, 0)),
+            ),
+            out_shape=jax.ShapeDtypeStruct((count, operators, spins, vector_count), jnp.float32),
+            compiler_params=pltpu.CompilerParams(vmem_limit_bytes=40 * MIB),
+            cost_estimate=pl.CostEstimate(
+                flops=1_070_000_000 * count, bytes_accessed=5_000_000 * count, transcendentals=0
+            ),
+            name="traces",
+        )(which, stacked, perambulators, products)
+
+    part_a = traces([back_4, early], [3, jnp.where(core == 0, 2, 0)])
+    part_b = traces([back_2, late], [1, jnp.where(core == 0, 0, 2)])
+    lines = jnp.stack(
+        [
+            jnp.where(core == 0, part_b[1], part_a[1]),
+            part_b[0],
+            jnp.where(core == 0, part_a[1], part_b[1]),
+            part_a[0],
+        ]
+    )
+    return jnp.sum(lines, axis=-1)
+
+
+def body_pair(vectors, links, momenta, displacements, perambulators):
+    vector_count = vectors.shape[2]
+    plane = LX * LY
+    depth = vectors.shape[3] // plane
+    blocks = lax.axis_size("space") // TG
+    block = lax.axis_index("space") // TG
+    planes = depth * blocks
+    rows = planes * LY
+    half = depth * LY
+    sites = planes * plane
+    operators = momenta.shape[0]
+    other_links = from_below(links)
+    own = jnp.transpose(vectors.reshape(COMPONENTS, vector_count, depth * plane), (0, 2, 1))
+    own = own.reshape(COMPONENTS, half, LX, vector_count)
+    other = from_below(own)
+
+    lattice = jnp.concatenate(
+        [links.reshape(54, depth, plane), other_links.reshape(54, depth, plane)], axis=1
+    )
+    lattice = jnp.transpose(lattice, (1, 0, 2))
+    lattice = jnp.concatenate(
+        [
+            lattice,
+            jnp.roll(lattice[:, 36:], 1, 0),
+            jnp.zeros((planes, 8, plane), jnp.bfloat16),
+        ],
+        axis=1,
+    )
+    pick, where, near = stencil_constants()
+    full, ahead = pl.pallas_call(
+        stencil_kernel,
+        in_specs=[VMEM] * 4,
+        out_specs=[VMEM] * 2,
+        out_shape=[
+            jax.ShapeDtypeStruct((rows, COMPONENTS * LX, USED), jnp.bfloat16),
+            jax.ShapeDtypeStruct((rows, COMPONENTS * LX, 8 * LX), jnp.bfloat16),
+        ],
+        compiler_params=pltpu.CompilerParams(vmem_limit_bytes=24 * MIB),
+        cost_estimate=pl.CostEstimate(flops=15_000_000_000, bytes_accessed=9_000_000, transcendentals=0),
+        name="stencil",
+    )(lattice, jnp.asarray(pick, jnp.bfloat16), where, near)
+
+    smeared, wide, moved = pl.pallas_call(
+        smear_kernel,
+        in_specs=[VMEM] * 4,
+        out_specs=[VMEM] * 3,
+        out_shape=[
+            jax.ShapeDtypeStruct((COMPONENTS, vector_count, depth * plane), jnp.bfloat16),
+            jax.ShapeDtypeStruct((vector_count, COMPONENTS * sites), jnp.bfloat16),
+            jax.ShapeDtypeStruct((3, COMPONENTS, rows, LX, vector_count), jnp.bfloat16),
+        ],
+        scratch_shapes=[pltpu.VMEM((COMPONENTS, rows, LX, vector_count), jnp.bfloat16)] * 3,
+        compiler_params=pltpu.CompilerParams(vmem_limit_bytes=36 * MIB),
+        cost_estimate=pl.CostEstimate(flops=5_000_000_000, bytes_accessed=16_000_000, transcendentals=0),
+        name="smear",
+    )(own, other, full, ahead)
+
+    x_frac = (momenta[:, 0:1] * lax.iota(jnp.int32, LX)[None] % LX).astype(jnp.float32) / LX
+    x_angle = jnp.broadcast_to((2.0 * math.pi * x_frac)[:, :, None], (operators, LX, vector_count))
+    row = lax.iota(jnp.int32, rows)[None]
+    coord_y = row % LY
+    coord_z = (row // LY + block * depth) % planes
+    row_angle = (momenta[:, 1:2] * coord_y % LY).astype(jnp.float32) / LY
+    row_angle = row_angle + (momenta[:, 2:3] * coord_z % planes).astype(jnp.float32) / planes
+    row_angle = 2.0 * math.pi * row_angle
+    scale = 1.0 / math.sqrt(sites)
+    pieces = []
+    chunk = operators
+    for offset in range(0, operators, chunk):
+        pieces.append(
+            pl.pallas_call(
+                functools.partial(elemental_kernel, offset, scale),
+                in_specs=[SMEM] * 3 + [VMEM] * 4,
+                out_specs=VMEM,
+                out_shape=jax.ShapeDtypeStruct((chunk, vector_count, 2 * vector_count), jnp.bfloat16),
+                scratch_shapes=[pltpu.VMEM((2, COMPONENTS * sites, 2 * vector_count), jnp.bfloat16)],
+                compiler_params=pltpu.CompilerParams(vmem_limit_bytes=30 * MIB),
+                cost_estimate=pl.CostEstimate(
+                    flops=400_000_000 * chunk, bytes_accessed=7_000_000, transcendentals=0
+                ),
+                name="elementals",
+            )(
+                displacements,
+                jnp.cos(row_angle),
+                jnp.sin(row_angle),
+                jnp.cos(x_angle),
+                jnp.sin(x_angle),
+                wide,
+                moved,
+            )
+        )
+    elem = pieces[0]
+    return (
+        smeared.reshape(2, 3, vector_count, depth * plane),
+        correlators(elem, perambulators),
+    )
+
+
 def solution(mesh):
     placed = (
         P(None, None, None, ("cfg", "space")),
@@ -263,8 +668,9 @@
         P(),
         P(None, None, None, ("cfg", "space")),
     )
+    blocks = mesh.shape["space"] // TG
     return jax.shard_map(
-        body,
+        body_pair if blocks == 2 else body_many,
         mesh=mesh,
         in_specs=placed,
         out_specs=(P(None, None, None, ("cfg", "space")), P(None, None, ("cfg", "space"))),

time: 460 us -> 150 us (0.33); the launches traced: 453 us -> 149 us
  local copies, waits for them, and re-layouts: 139 us -> 6.14 us
  other arithmetic: 102 us -> 4.57 us
  Pallas kernels: 0 us -> 73.1 us
  matrix products: 65 us -> 0 us
  waiting for transfers between devices: 116 us -> 57.9 us
  loops' own time: 16.4 us -> 0 us
  between operations: 5.65 us -> 0.8 us
    pallas_call x0 -> x6, Pallas kernels: none -> 73.1 us  [the longest x1 19.8 us: body_pair(): pl.pallas_call(stencil_kernel, in_specs=[VMEM] * 4, out_specs=[VMEM] * 2,...]
    dot_general x36 -> x0, matrix products: 65 us -> none  [the longest x4 14.7 us: body(): jnp.einsum('asp,masl->mspl', tau_re3, product[:, :, 1], preferred_element...]
    unnamed x656 -> x11, local copies, waits for them, and re-layouts: 55.3 us -> 3.44 us
    ppermute x9 -> x2, waiting for transfers between devices: 85.5 us -> 34.6 us  [passed_along(): lax.ppermute(shard, axis, [(i, (i + by) % peers) for i in range(peers)])]
    slice x70 -> x3, local copies, waits for them, and re-layouts: 48 us -> 0.82 us  [the longest x1 0.8 us: body_pair(): momenta[:, 0:1] * lax.iota(jnp.int32, LX)[None] % LX]
    another operation x49 -> x4, other arithmetic: 46.2 us -> 2.43 us  [the longest x2 2.28 us: traces(): stacked = jnp.stack(sources)]
    cos x8 -> x0, other arithmetic: 16.8 us -> none  [operator(): cosine = jnp.cos(angle)]
    another operation x1 -> x0, loops' own time: 16.4 us -> none  [body(): partial_sum = lax.map(operator, (momenta, displacements))]
  transfers between devices with their start and end apart: 11 -> 6, of which waited for: 8 -> 3; matrix products, arithmetic and copies ran while one was open for 29% -> 2% of each run, Pallas kernels for 0% -> 24%
where the time goes in v1:
time: 150 us; the launch traced here: 149 us
  Pallas kernels  73.1 us (49%)
  waiting for transfers between devices  57.9 us (39%)
  starting transfers between devices  6.43 us (4%)
  local copies, waits for them, and re-layouts  6.14 us (4%)
  other arithmetic  4.57 us (3%)
    ppermute x2, waiting for transfers between devices, passed_along(): lax.ppermute(shard, axis, [(i, (i + by) % peers) for i in range(peers)])  34.6 us
    ppermute x4, waiting for transfers between devices, partner_2(): lax.ppermute(shard, axis, [(i, i ^ 1 << apart) for i in range(lax.axis_si...  23.3 us
    pallas_call x1, Pallas kernels, body_pair(): pl.pallas_call(stencil_kernel, in_specs=[VMEM] * 4, out_specs=[VMEM] * 2,...  19.8 us
    pallas_call x1, Pallas kernels, body_pair(): pl.pallas_call(functools.partial(elemental_kernel, offset, scale), in_spe...  16 us
    pallas_call x2, Pallas kernels, traces(): pl.pallas_call(trace_kernel, grid_spec=pltpu.PrefetchScalarGridSpec(num_s...  15.8 us
    pallas_call x1, Pallas kernels, body_pair(): pl.pallas_call(smear_kernel, in_specs=[VMEM] * 4, out_specs=[VMEM] * 3, o...  13.7 us
    pallas_call x1, Pallas kernels, correlators(): pl.pallas_call(right_kernel, grid=(HOPS,), in_specs=[pl.BlockSpec((operat...  7.73 us
    ppermute x2, starting transfers between devices, passed_along(): lax.ppermute(shard, axis, [(i, (i + by) % peers) for i in range(peers)])  4.21 us
  transfers between devices with their start and end apart: 6, of which 3 were waited for; matrix products, arithmetic and copies ran while one was open for 2% of the time, Pallas kernels for 24%

profile of v1, /device:TPU:0, one launch (start us, length us, event | category | flops | bytes accessed | tf_op | source)
XLA Modules:
  0.0 149.0 jit_solution(3042038808162513810)
XLA Ops:
  0.6 1.5 %copy.11 = bf16[6,128,512]{1,2,0:T(8,128)(2,1)S(1)} copy(bf16[6,128,512]{2,1,0:T(8,128)(2,1)} %bitcast.22) | data formatting | bytes 1572864 | tf_op jit(solution)/shard_map/reshape | solution.py:577
  2.1 4.1 %collective-permute-start = (bf16[6,32,16,128]{3,2,1,0:T(8,128)(2,1)S(1)}, bf16[6,32,16,128]{3,2,1,0:T(8,128)(2,1)S(1)}, u32[]{:S(2)}, u32[]{:S(2)}) collective-permute-start(bf16[6,32,16,128]{3,2,1,0:T(8,128)(2,1)S(1)} %bitcast.19), channel_id=1, source_target_pairs={{0,8},{1,9},{2,10},{3,11},{4,12},{5,13},{6,14},{7,15},{8,0},{9,1},... | collective-permute-start | bytes 2359304 | tf_op jit(solution)/shard_map/ppermute | solution.py:23
  6.3 0.1 collective-permute-start.1
  6.4 0.8 slice_bitcast_fusion
  7.2 0.1 fusion.16
  7.3 0.1 fusion.14
  7.4 0.8 copy.12
  8.3 0.1 reshape.127
  8.3 0.1 pad.15.clone
  8.4 34.6 %collective-permute-done.1 = bf16[3,2,3,3,512]{4,1,3,2,0:T(2,128)(2,1)S(1)} collective-permute-done((bf16[3,2,3,3,512]{4,1,3,2,0:T(2,128)(2,1)}, bf16[3,2,3,3,512]{4,1,3,2,0:T(2,128)(2,1)S(1)}, u32[]{:S(2)}, u32[]{:S(2)}) %collective-permute-start.1) | collective-permute-done | bytes 55328 | tf_op jit(solution)/shard_map/ppermute | solution.py:23
  43.1 0.1 reshape.128
  43.2 0.1 maximum_maximum_fusion.links_ref
  43.3 0.0 copy-start.2
  43.3 1.1 copy-done.2
  44.4 0.0 copy-start.3
  44.4 0.8 copy-done.3
  45.2 0.0 copy-start.4
  45.2 0.7 copy-done.4
  45.9 19.8 %stencil.1 = (bf16[64,96,512]{2,1,0:T(8,128)(2,1)S(1)}, bf16[64,96,128]{2,1,0:T(8,128)(2,1)S(1)}) custom-call(bf16[4,80,256]{2,1,0:T(8,128)(2,1)S(1)} %maximum_maximum_fusion.links_ref, bf16[6,80,640]{2,1,0:T(8,128)(2,1)S(1)} %copy-done.2, s32[8,640]{1,0:T(8,128)S(1)} %copy-done.4, f32[16,640]{1,0:T(8,128)S(1)} %copy-done.3), custom_call_target="tpu_custom_call" | custom-call | flops 15000000512 | bytes 9000000 | tf_op jit(solution)/shard_map/stencil/pallas_call | solution.py:594
  65.7 0.0 collective-permute-done.other_ref
  65.7 0.0 copy-start.1
  65.7 13.7 %smear.1 = (bf16[6,128,512]{2,1,0:T(8,128)(2,1)}, bf16[128,6144]{1,0:T(8,128)(2,1)S(1)}, bf16[3,6,64,16,128]{4,3,2,1,0:T(8,128)(2,1)S(1)}) custom-call(bf16[6,32,16,128]{3,2,1,0:T(8,128)(2,1)S(1)} %bitcast.20, bf16[6,32,16,128]{3,2,1,0:T(8,128)(2,1)S(1)} %collective-permute-done.other_ref, bf16[64,96,512]{2,1,0:T(8,128)(2,1)S(1)} %get-tuple-element.7.full_ref, ...), custom_call_target="tpu_custom_call" | custom-call | flops 5000000000 | bytes 16000000 | tf_op jit(solution)/shard_map/smear/pallas_call | solution.py:607
  79.4 0.1 broadcast_in_dim.14.cos_ref
  79.5 0.1 broadcast_in_dim.15.sin_ref
  79.6 0.0 copy-done.1
  79.6 0.0 copy-start
  79.6 16.0 %elementals.1.elem_ref = bf16[8,128,256]{2,1,0:T(8,128)(2,1)S(1)} custom-call(s32[8]{0:T(128)S(1)} %copy-done.1, f32[8,64]{1,0:T(8,128)S(1)} %get-tuple-element.22.row_cos_ref, f32[8,64]{1,0:T(8,128)S(1)} %get-tuple-element.21.row_sin_ref, f32[8,16,128]{2,1,0:T(8,128)S(1)} %broadcast_in_dim.14.cos_ref, f32[8,16,128]{2,1,0:T(8,128)S(1)} %broadcast_in_dim.15.sin_ref, ...), custom_call_target="tpu_custom_call" | custom-call | flops 3200000000 | bytes 7000000 | tf_op jit(solution)/shard_map/elementals/pallas_call | solution.py:635
  95.6 0.9 collective-permute-start.2
  96.5 12.3 %collective-permute-done.2 = bf16[8,128,256]{2,1,0:T(8,128)(2,1)S(1)} collective-permute-done((bf16[8,128,256]{2,1,0:T(8,128)(2,1)S(1)}, bf16[8,128,256]{2,1,0:T(8,128)(2,1)S(1)}, u32[]{:S(2)}, u32[]{:S(2)}) %collective-permute-start.2) | collective-permute-done | bytes 524320 | tf_op jit(solution)/shard_map/ppermute | solution.py:27
  108.8 1.0 broadcast_select_fusion.1
  109.8 1.3 collective-permute-start.3
  111.2 0.0 collective-permute-start.5
  111.2 0.1 pad_add_fusion.1.which_ref
  111.2 0.1 pad_add_fusion.which_ref
  111.3 11.1 %collective-permute-done.3 = bf16[8,128,256]{2,1,0:T(8,128)(2,1)} collective-permute-done((bf16[8,128,256]{2,1,0:T(8,128)(2,1)}, bf16[8,128,256]{2,1,0:T(8,128)(2,1)}, u32[]{:S(2)}, u32[]{:S(2)}) %collective-permute-start.3) | collective-permute-done | bytes 524320 | tf_op jit(solution)/shard_map/ppermute | solution.py:27
  122.4 0.0 collective-permute-start.4
  122.4 0.0 copy-done
  122.4 7.7 %right.1.product_ref = bf16[4,8,1024,256]{3,2,1,0:T(8,128)(2,1)} custom-call(bf16[8,128,256]{2,1,0:T(8,128)(2,1)S(1)} %elementals.1.elem_ref, bf16[4,2,128,1024]{3,2,1,0:T(8,128)(2,1)S(1)} %copy-done), custom_call_target="tpu_custom_call" | custom-call | flops 4300000256 | bytes 20000000 | tf_op jit(solution)/shard_map/right/pallas_call | solution.py:517
  130.1 0.0 collective-permute-done.5
  130.1 1.1 pad_maximum_fusion.1.source_ref
  131.3 7.9 %traces.3 = f32[2,8,8,128]{3,2,1,0:T(8,128)S(1)} custom-call(s32[2]{0:T(128)S(1)} %pad_add_fusion.1.which_ref, bf16[2,8,128,256]{3,2,1,0:T(8,128)(2,1)S(1)} %pad_maximum_fusion.1.source_ref, bf16[4,2,128,1024]{3,2,1,0:T(8,128)(2,1)S(1)} %copy-done, bf16[4,8,1024,256]{3,2,1,0:T(8,128)(2,1)} %right.1.product_ref), custom_call_target="tpu_custom_call" | custom-call | flops 2140000000 | bytes 10000000 | tf_op jit(solution)/shard_map/traces/pallas_call | solution.py:532
  139.2 0.0 collective-permute-done.4
  139.2 1.1 pad_maximum_fusion.source_ref
  140.4 7.9 %traces.2 = f32[2,8,8,128]{3,2,1,0:T(8,128)S(1)} custom-call(s32[2]{0:T(128)S(1)} %pad_add_fusion.which_ref, bf16[2,8,128,256]{3,2,1,0:T(8,128)(2,1)S(1)} %pad_maximum_fusion.source_ref, bf16[4,2,128,1024]{3,2,1,0:T(8,128)(2,1)S(1)} %copy-done, bf16[4,8,1024,256]{3,2,1,0:T(8,128)(2,1)} %right.1.product_ref), custom_call_target="tpu_custom_call" | custom-call | flops 2140000000 | bytes 10000000 | tf_op jit(solution)/shard_map/traces/pallas_call | solution.py:532
  148.3 0.7 maximum_reduce_fusion
  (9 shorter events, 0.1 us)
Async XLA Ops:
  2.1 63.6 %collective-permute-start = (bf16[6,32,16,128]{3,2,1,0:T(8,128)(2,1)S(1)}, bf16[6,32,16,128]{3,2,1,0:T(8,128)(2,1)S(1)}, u32[]{:S(2)}, u32[]{:S(2)}) collective-permute-start(bf16[6,32,16,128]{3,2,1,0:T(8,128)(2,1)S(1)} %bitcast.19), channel_id=1, source_target_pairs={{0,8},{1,9},{2,10},{3,11},{4,12},{5,13},{6,14},{7,15},{8,0},{9,1},... | collective-permute-start | bytes 2359304 | tf_op jit(solution)/shard_map/ppermute | solution.py:23
  6.3 36.8 %collective-permute-start.1 = (bf16[3,2,3,3,512]{4,1,3,2,0:T(2,128)(2,1)}, bf16[3,2,3,3,512]{4,1,3,2,0:T(2,128)(2,1)S(1)}, u32[]{:S(2)}, u32[]{:S(2)}) collective-permute-start(bf16[3,2,3,3,512]{4,1,3,2,0:T(2,128)(2,1)} %param.9), channel_id=1, source_target_pairs={{0,8},{1,9},{2,10},{3,11},{4,12},{5,13},{6,14},{7,15},{8,0},{9,1},... | collective-permute-start | bytes 165896 | tf_op jit(solution)/shard_map/ppermute | solution.py:23
  43.3 1.1 copy-start.2
  44.4 0.8 copy-start.3
  45.2 0.7 copy-start.4
  65.7 13.9 %copy-start.1 = (s32[8]{0:T(128)S(1)}, s32[8]{0:T(128)}, u32[]{:S(2)}) copy-start(s32[8]{0:T(128)} %direction_ref.1) | copy-start | bytes 100
  79.6 42.8 %copy-start = (bf16[4,2,128,1024]{3,2,1,0:T(8,128)(2,1)S(1)}, bf16[4,2,128,1024]{3,2,1,0:T(8,128)(2,1)}, u32[]{:S(2)}) copy-start(bf16[4,2,128,1024]{3,2,1,0:T(8,128)(2,1)} %tau_ref.5) | copy-start | bytes 6291460
  95.6 13.1 %collective-permute-start.2 = (bf16[8,128,256]{2,1,0:T(8,128)(2,1)S(1)}, bf16[8,128,256]{2,1,0:T(8,128)(2,1)S(1)}, u32[]{:S(2)}, u32[]{:S(2)}) collective-permute-start(bf16[8,128,256]{2,1,0:T(8,128)(2,1)S(1)} %elementals.1.elem_ref), channel_id=1, source_target_pairs={{0,4},{1,5},{2,6},{3,7},{4,0},{5,1},{6,2},{7,3},{8,12},{9,13},{10,... | collective-permute-start | bytes 1572872 | tf_op jit(solution)/shard_map/ppermute | solution.py:27
  109.8 12.5 %collective-permute-start.3 = (bf16[8,128,256]{2,1,0:T(8,128)(2,1)}, bf16[8,128,256]{2,1,0:T(8,128)(2,1)}, u32[]{:S(2)}, u32[]{:S(2)}) collective-permute-start(bf16[8,128,256]{2,1,0:T(8,128)(2,1)} %get-tuple-element.12), channel_id=1, source_target_pairs={{0,2},{1,3},{2,0},{3,1},{4,6},{5,7},{6,4},{7,5},{8,10},{9,11},{10,... | collective-permute-start | bytes 1572872 | tf_op jit(solution)/shard_map/ppermute | solution.py:27
  111.2 18.9 %collective-permute-start.5 = (bf16[8,128,256]{2,1,0:T(8,128)(2,1)}, bf16[8,128,256]{2,1,0:T(8,128)(2,1)}, u32[]{:S(2)}, u32[]{:S(2)}) collective-permute-start(bf16[8,128,256]{2,1,0:T(8,128)(2,1)} %get-tuple-element.13), channel_id=1, source_target_pairs={{0,1},{1,0},{2,3},{3,2},{4,5},{5,4},{6,7},{7,6},{8,9},{9,8},{10,11... | collective-permute-start | bytes 1572872 | tf_op jit(solution)/shard_map/ppermute | solution.py:27
  122.4 16.8 %collective-permute-start.4 = (bf16[8,128,256]{2,1,0:T(8,128)(2,1)}, bf16[8,128,256]{2,1,0:T(8,128)(2,1)S(1)}, u32[]{:S(2)}, u32[]{:S(2)}) collective-permute-start(bf16[8,128,256]{2,1,0:T(8,128)(2,1)} %collective-permute-done.3), channel_id=1, source_target_pairs={{0,1},{1,0},{2,3},{3,2},{4,5},{5,4},{6,7},{7,6},{8,9},{9,8},{10,11... | collective-permute-start | bytes 1572872 | tf_op jit(solution)/shard_map/ppermute | solution.py:27
